TPU v7x, 512 devices: a whole 4x4x16 slice. The times are simulated.
512 devices in a mesh: rows: 64 (over y, z), cols: 8 (over x, core).
Axes of the slice: x: 4, y: 4, z: 16, core: 2. Of those that a mesh axis runs over, the one named last changes fastest.
Arguments:
- images: float32 [512, 32, 128], P('rows'), may hold values from -6 to 6
- gauge_pixel: int32 [131072], P('rows'), may hold values from 0 to 32767
- row_mask: int32 [131072], P('rows'), may hold values 0 or 1
- gauge_counts: int32 [64], P('rows'), may hold values from 1 to 2048, as said below
- targets: float32 [131072], P('rows'), may hold values from -10 to 10
- theta: float32 [64, 8], replicated, may hold values from -2.5 to 2.5
- amplitude: float32 [64], replicated, may hold values from 0.5 to 1.5
- damping: float32 [], replicated, may hold values from 0.05 to 0.3
Outputs:
- r_factor: float32 [512, 512], replicated
- new_theta: float32 [64, 8], replicated
- predicted: float32 [131072], P(('rows', 'cols'))
Inputs may be any that keep to these rules, and one draw needn't show every extreme that they name: The slots in use on an index of rows are its first gauge_counts slots; one index of rows uses all 2048.
All inputs are finite; a program needn't handle non-finite values. No bound on the sum of `row_mask` on one device may be relied on, other than what follows from the above.
Results may differ from a plain program's by a relative error of at most 0.0003.
Values sent between devices are 32-bit elements; how exact they have to be, the bound alone decides.
A program may use at most 64 MiB of HBM per device.

v0:
```python
import jax
import jax.numpy as jnp
from jax import lax
from jax.sharding import PartitionSpec as P

BLOCK = 256
y_orders = [0, 1, 0, 2, 1, 0, 0, 0]
x_orders = [0, 0, 1, 0, 1, 2, 0, 2]
sigmas = [1.5, 1.5, 1.5, 1.5, 1.5, 1.5, 3.0, 3.0]


def kernel_values(spacing, deriv_order, width_sigma):
    envelope = jnp.exp(-spacing * spacing / (2.0 * width_sigma * width_sigma))
    if deriv_order == 1:
        return -spacing / width_sigma**2 * envelope
    if deriv_order == 2:
        return (spacing * spacing / width_sigma**4 - 1.0 / width_sigma**2) * envelope
    return envelope


def kernel_table(length, deriv_order, width_sigma):
    places = jnp.arange(length)
    spacing = (places[:, None] - places[None, :]).astype(jnp.float32)
    sample = jnp.arange(-12, 13).astype(jnp.float32)
    scaling = jnp.sqrt(jnp.sum(kernel_values(sample, deriv_order, width_sigma) ** 2))
    return kernel_values(spacing, deriv_order, width_sigma) / scaling


def features(clip_tiles):
    height = clip_tiles.shape[1]
    breadth = clip_tiles.shape[2]
    left_tabs = jnp.stack(
        [kernel_table(height, y_orders[which], sigmas[which]) for which in range(8)]
    )
    right_tabs = jnp.stack(
        [kernel_table(breadth, x_orders[which], sigmas[which]) for which in range(8)]
    )
    partial_conv = jnp.einsum(
        "kij,cjw->kciw", left_tabs, clip_tiles, precision=lax.Precision.HIGHEST
    )
    full_conv = jnp.einsum(
        "kciw,kvw->kciv", partial_conv, right_tabs, precision=lax.Precision.HIGHEST
    )
    return full_conv.reshape(full_conv.shape[0], -1)


def outer_rows(slope, phi):
    return (slope[:, :, None] * phi[:, None, :]).reshape(slope.shape[0], -1)


def solve_step(lower, rhs):
    inner = lax.linalg.triangular_solve(lower, rhs[:, None], left_side=True, lower=True)
    outer = lax.linalg.triangular_solve(lower, inner, left_side=True, lower=True, transpose_a=True)
    return -outer[:, 0]


def on_device(images, gauge_pixel, row_mask, gauge_counts, targets, theta, amplitude, damping):
    ncols = lax.axis_size("cols")
    column = lax.axis_index("cols")
    slots = gauge_pixel.shape[0]
    share = slots // ncols
    channels = theta.shape[0]
    basis_count = theta.shape[1]
    params = channels * basis_count
    local_width = channels // ncols
    own_params = local_width * basis_count
    count = gauge_counts[0]
    live = ((jnp.arange(slots) < count) & (row_mask == 1)).astype(jnp.float32)
    flat_feats = features(images)
    phi = jnp.take(flat_feats, gauge_pixel, axis=1).T
    act = jnp.tanh(jnp.dot(phi, theta.T, precision=lax.Precision.HIGHEST))
    model = jnp.dot(act, amplitude, precision=lax.Precision.HIGHEST)
    resid = live * (model - targets)
    slope = live[:, None] * amplitude[None, :] * (1.0 - act * act)

    def block_rows(values):
        return lax.dynamic_slice_in_dim(values, column * share, share, 0)

    def pick(values):
        return block_rows(values)

    local_slope = lax.dynamic_slice_in_dim(slope, column * local_width, local_width, 1)
    jac_cols = outer_rows(local_slope, phi)
    prefix = jnp.clip(count - column * share, 0, share)
    assigned = lax.all_to_all(jac_cols, "cols", split_axis=0, concat_axis=1, tiled=True)
    assigned_resid = pick(resid)
    trips = (prefix + BLOCK - 1) // BLOCK

    def add_block(which, carry):
        gram = carry[0] + lax.dot_general(
            assigned,
            assigned,
            (((0,), (0,)), ((), ())),
            precision=lax.Precision.HIGHEST,
            preferred_element_type=jnp.float32,
        )
        grad = carry[1] + jnp.dot(assigned_resid, assigned, precision=lax.Precision.HIGHEST)
        return (gram, grad)

    start = (jnp.zeros((params, params), jnp.float32), jnp.zeros((params,), jnp.float32))
    gram_part, grad_part = lax.fori_loop(0, trips, add_block, start)
    live_part = jnp.sum(pick(live))
    gram, grad, total = lax.psum((gram_part, grad_part, live_part), ("rows", "cols"))
    normal = gram / total + damping * jnp.eye(params, dtype=jnp.float32)
    lower = jnp.linalg.cholesky(normal)
    step = solve_step(lower, grad / total)
    local_step = lax.dynamic_slice_in_dim(step, column * own_params, own_params, 0)
    linear_part = lax.psum_scatter(
        jnp.dot(jac_cols, local_step, precision=lax.Precision.HIGHEST),
        "cols",
        scatter_dimension=0,
        tiled=True,
    )
    predicted = block_rows(resid) + linear_part
    return (lower.T, theta + step.reshape(channels, basis_count), predicted)


def solution(mesh):
    return jax.shard_map(
        on_device,
        mesh=mesh,
        in_specs=(P("rows", None, None), P("rows"), P("rows"), P("rows"), P("rows"), P(), P(), P()),
        out_specs=(P(), P(), P(("rows", "cols"))),
        check_vma=False,
    )
```

profile of v0, /device:TPU:8, one launch (start us, length us, event | category | flops | bytes accessed | tf_op | source)
XLA Modules:
  0.0 705.4 jit_solution(6471413244750945603)
XLA Ops:
  18.4 8.6 %copy.61 = f32[8,8,32,128]{0,3,2,1:T(8,128)} copy(f32[8,8,32,128]{3,2,1,0:T(8,128)S(1)} %fusion.15) | data formatting | bytes 2097152 | tf_op jit(solution)/shard_map/reshape | solution.py:44
  27.0 11.2 %gather_fusion = f32[2048,8]{1,0:T(8,128)S(1)} fusion(f32[8,32768]{0,1:T(8,128)} %bitcast.185, s32[2048]{0:T(1024)S(1)} %fusion.50), kind=kCustom, calls=%fused_computation | custom fusion | bytes 139264 | tf_op jit(solution)/shard_map/jit(_take)/gather | solution.py:70
  38.8 1.3 convolution_tanh_fusion
  41.5 4.3 all-to-all-start
  47.1 9.1 %all-to-all-done = f32[8,256,64]{1,2,0:T(8,128)S(1)} async-done(((f32[8,256,64]{1,2,0:T(8,128)}), f32[8,256,64]{1,2,0:T(8,128)S(1)}, u32[]{:S(2)}, u32[]{:S(2)}) %all-to-all-start) | async-done | bytes 524320 | tf_op jit(solution)/shard_map/all_to_all | solution.py:85
  58.2 1.3 copy.45
  62.9 108.7 %all-reduce.2 = (f32[]{:T(128)}, f32[512]{0:T(512)S(1)}) all-reduce(f32[]{:T(128)} %dynamic-slice_reduce_fusion, f32[512]{0:T(512)S(1)} %get-tuple-element.82), channel_id=1, replica_groups=mesh['rows'=64,'cols'=8] {'rows','cols'}, use_global_device_ids=true, to_apply=%region_9.0 | all-reduce | flops 513 | bytes 4104 | tf_op jit(solution)/shard_map/psum | solution.py:103
  172.3 363.3 %all-reduce.5.cloned.1.call-done = f32[512,512]{0,1:T(8,128)} async-done(((f32[512,512]{0,1:T(8,128)}), f32[512,512]{0,1:T(8,128)}) %all-reduce.5.cloned.1.call-update) | async-done | bytes 1048592 | tf_op jit(solution)/shard_map/psum | solution.py:103
  535.6 2.0 select_add_fusion
  537.9 2.1 fusion.12
  540.1 11.7 %cholesky.103 = f32[128,128]{1,0:T(8,128)S(1)} custom-call(f32[128,128]{1,0:T(8,128)S(1)} %cholesky.263), custom_call_target="Cholesky" | custom-call | tf_op jit(solution)/shard_map/jit(cholesky)/cholesky | solution.py:105
  551.8 9.8 %custom-call.32 = f32[1,128,128]{1,2,0:T(8,128)S(1)} custom-call(f32[1,128,128]{2,1,0:T(8,128)S(1)} %get-tuple-element.162), custom_call_target="InvertDiagBlocksLowerTriangular" | custom-call | tf_op jit(solution)/shard_map/jit(cholesky)/cholesky | solution.py:105
  562.3 11.7 %cholesky.215 = f32[128,128]{1,0:T(8,128)S(1)} custom-call(f32[128,128]{1,0:T(8,128)S(1)} %cholesky.267), custom_call_target="Cholesky" | custom-call | tf_op jit(solution)/shard_map/jit(cholesky)/cholesky | solution.py:105
  574.5 9.9 %custom-call.33 = f32[1,128,128]{1,2,0:T(8,128)S(1)} custom-call(f32[1,128,128]{2,1,0:T(8,128)S(1)} %get-tuple-element.160), custom_call_target="InvertDiagBlocksLowerTriangular" | custom-call | tf_op jit(solution)/shard_map/jit(cholesky)/cholesky | solution.py:105
  585.5 11.7 %cholesky.236 = f32[128,128]{1,0:T(8,128)S(1)} custom-call(f32[128,128]{1,0:T(8,128)S(1)} %cholesky.272), custom_call_target="Cholesky" | custom-call | tf_op jit(solution)/shard_map/jit(cholesky)/cholesky | solution.py:105
  597.3 9.8 %custom-call.34 = f32[1,128,128]{1,2,0:T(8,128)S(1)} custom-call(f32[1,128,128]{2,1,0:T(8,128)S(1)} %get-tuple-element.158), custom_call_target="InvertDiagBlocksLowerTriangular" | custom-call | tf_op jit(solution)/shard_map/jit(cholesky)/cholesky | solution.py:105
  607.9 11.9 %cholesky.253 = f32[128,128]{1,0:T(8,128)S(1)} custom-call(f32[128,128]{1,0:T(8,128)S(1)} %convolution_subtract_fusion.2), custom_call_target="Cholesky" | custom-call | tf_op jit(solution)/shard_map/jit(cholesky)/cholesky | solution.py:105
  625.8 11.3 %while.16 = (s32[]{:T(128)}, f32[512,512]{0,1:T(8,128)S(1)}, s32[4,2]{0,1:T(2,128)S(1)}, f32[4,128,128]{2,1,0:T(8,128)}, s32[]{:T(128)}) while((s32[]{:T(128)}, f32[512,512]{0,1:T(8,128)S(1)}, s32[4,2]{0,1:T(2,128)S(1)}, f32[4,128,128]{2,1,0:T(8,128)}, s32[]{:T(128)}) %tuple.61), condition=%wide.while_cond, body=%wide.while_body.sunk | while | flops 2 | bytes 393829 | solution.py:53
  626.4 1.4 dynamic-slice.12
  629.3 1.4 dynamic-slice.12
  632.1 1.4 dynamic-slice.12
  634.9 1.4 dynamic-slice.12
  637.1 40.1 %custom-call.35 = f32[4,128,128]{1,2,0:T(8,128)S(1)} custom-call(f32[4,128,128]{2,1,0:T(8,128)} %get-tuple-element.90), custom_call_target="InvertDiagBlocksLowerTriangular" | custom-call | tf_op jit(solution)/shard_map/triangular_solve | solution.py:53
  681.7 15.2 %all-reduce.1 = f32[2048]{0:T(1024)S(1)} all-reduce(f32[2048]{0:T(1024)S(1)} %bitcast.197), channel_id=2, replica_groups=mesh['rows'=64,'cols'=8] {'cols'}, use_global_device_ids=true, to_apply=%region_19.20.clone | all-reduce | flops 2048 | bytes 16384
  (124 shorter events, 33.4 us)
Async XLA Ops:
  7.2 9.1 %copy-start = (f32[8,32,128]{2,1,0:T(8,128)S(1)}, f32[8,32,128]{2,1,0:T(8,128)}, u32[]{:S(2)}) copy-start(f32[8,32,128]{2,1,0:T(8,128)} %param.10) | copy-start | bytes 393220
  7.2 31.7 %copy-start.1 = (f32[64,8]{0,1:T(8,128)S(1)}, f32[64,8]{0,1:T(8,128)}, u32[]{:S(2)}) copy-start(f32[64,8]{0,1:T(8,128)} %param.15) | copy-start | bytes 6148
  7.2 33.0 %copy-start.3 = (f32[64]{0:T(128)S(1)}, f32[64]{0:T(128)}, u32[]{:S(2)}) copy-start(f32[64]{0:T(128)} %param.16) | copy-start | bytes 772
  7.2 33.1 %copy-start.2 = (s32[2048]{0:T(1024)S(1)}, s32[2048]{0:T(1024)}, u32[]{:S(2)}) copy-start(s32[2048]{0:T(1024)} %param.12) | copy-start | bytes 24580
  41.5 14.6 %all-to-all-start = ((f32[8,256,64]{1,2,0:T(8,128)}), f32[8,256,64]{1,2,0:T(8,128)S(1)}, u32[]{:S(2)}, u32[]{:S(2)}) async-start(f32[8,256,64]{1,2,0:T(8,128)} %copy.43), calls=%async_computation | async-start | bytes 1048576 | tf_op jit(solution)/shard_map/all_to_all | solution.py:85
  45.8 489.8 %all-reduce.5.cloned.1.call-start = ((), (), s32[]{:S(2)}) async-start(), calls=%async_computation.1 | async-start | bytes 2097152 | tf_op jit(solution)/shard_map/psum | solution.py:103
Sparse Core Ops, SparseCore 0:
  59.6 475.9 all-reduce.4
where the time goes:
time: 712 us; the launch traced here: 705 us
  waiting for transfers between devices  372 us (52%)
  other arithmetic  133 us (19%)
  blocking collectives  124 us (17%)
  local copies, waits for them, and re-layouts  37.7 us (5%)
  between operations  22.7 us (3%)
  matrix products  10.9 us (2%)
    psum x1, waiting for transfers between devices, on_device(): lax.psum((gram_part, grad_part, live_part), ('rows', 'cols'))  363 us
    psum x1, blocking collectives, on_device(): lax.psum((gram_part, grad_part, live_part), ('rows', 'cols'))  109 us
    another operation x14, other arithmetic, on_device(): lower = jnp.linalg.cholesky(normal)  78.7 us
    another operation x3, other arithmetic, solve_step(): lax.linalg.triangular_solve(lower, inner, left_side=True, lower=True, tra...  41.4 us
    unnamed x1, blocking collectives  15.2 us
  transfers between devices with their start and end apart: 2, of which 2 were waited for; matrix products, arithmetic and copies ran while one was open for 1% of the time, Pallas kernels for 0%

commit v1 on v0

--- a/solution.py
+++ b/solution.py
@@ -100,7 +100,9 @@
     start = (jnp.zeros((params, params), jnp.float32), jnp.zeros((params,), jnp.float32))
     gram_part, grad_part = lax.fori_loop(0, trips, add_block, start)
     live_part = jnp.sum(pick(live))
-    gram, grad, total = lax.psum((gram_part, grad_part, live_part), ("rows", "cols"))
+    gram, grad, total = jax.lax.psum(
+        jax.lax.psum((gram_part, grad_part, live_part), "cols"), "rows"
+    )
     normal = gram / total + damping * jnp.eye(params, dtype=jnp.float32)
     lower = jnp.linalg.cholesky(normal)
     step = solve_step(lower, grad / total)

time: 712 us -> 594 us (0.83)
  the two profiles are of different devices: /device:TPU:8 before, /device:TPU:1 now
where the time goes in v1:
time: 594 us; the launch traced here: 587 us
  waiting for transfers between devices  218 us (37%)
  blocking collectives  154 us (26%)
  other arithmetic  133 us (22%)
  local copies, waits for them, and re-layouts  37.7 us (6%)
  between operations  22.7 us (4%)
  matrix products  10.9 us (2%)
  starting transfers between devices  10.3 us (2%)
    psum x1, waiting for transfers between devices, on_device(): jax.lax.psum(jax.lax.psum((gram_part, grad_part, live_part), 'cols'), 'ro...  135 us
    psum x1, blocking collectives, on_device(): jax.lax.psum(jax.lax.psum((gram_part, grad_part, live_part), 'cols'), 'ro...  117 us
    another operation x14, other arithmetic, on_device(): lower = jnp.linalg.cholesky(normal)  78.7 us
    psum x1, waiting for transfers between devices, on_device(): jax.lax.psum((gram_part, grad_part, live_part), 'cols')  74.9 us
    another operation x3, other arithmetic, solve_step(): lax.linalg.triangular_solve(lower, inner, left_side=True, lower=True, tra...  41.4 us
    unnamed x1, blocking collectives  22.7 us
    psum x1, blocking collectives, on_device(): jax.lax.psum((gram_part, grad_part, live_part), 'cols')  14.6 us
  transfers between devices with their start and end apart: 3, of which 3 were waited for; matrix products, arithmetic and copies ran while one was open for 1% of the time, Pallas kernels for 0%

profile of v1, /device:TPU:1, one launch (start us, length us, event | category | flops | bytes accessed | tf_op | source)
XLA Modules:
  0.0 587.3 jit_solution(17321946728605778132)
XLA Ops:
  18.4 8.6 %copy.61 = f32[8,8,32,128]{0,3,2,1:T(8,128)} copy(f32[8,8,32,128]{3,2,1,0:T(8,128)S(1)} %fusion.15) | data formatting | bytes 2097152 | tf_op jit(solution)/shard_map/reshape | solution.py:44
  27.0 11.2 %gather_fusion = f32[2048,8]{1,0:T(8,128)S(1)} fusion(f32[8,32768]{0,1:T(8,128)} %bitcast.185, s32[2048]{0:T(1024)S(1)} %fusion.50), kind=kCustom, calls=%fused_computation | custom fusion | bytes 139264 | tf_op jit(solution)/shard_map/jit(_take)/gather | solution.py:70
  41.5 10.2 %all-to-all-start = ((f32[8,256,64]{1,2,0:T(8,128)}), f32[8,256,64]{1,2,0:T(8,128)S(1)}, u32[]{:S(2)}, u32[]{:S(2)}) async-start(f32[8,256,64]{1,2,0:T(8,128)} %copy.43), calls=%async_computation | async-start | bytes 1048576 | tf_op jit(solution)/shard_map/all_to_all | solution.py:85
  52.9 8.2 %all-to-all-done = f32[8,256,64]{1,2,0:T(8,128)S(1)} async-done(((f32[8,256,64]{1,2,0:T(8,128)}), f32[8,256,64]{1,2,0:T(8,128)S(1)}, u32[]{:S(2)}, u32[]{:S(2)}) %all-to-all-start) | async-done | bytes 524320 | tf_op jit(solution)/shard_map/all_to_all | solution.py:85
  64.6 74.9 %all-reduce.7.cloned.1.call-done = f32[512,512]{0,1:T(8,128)} async-done(((f32[512,512]{0,1:T(8,128)}), f32[512,512]{0,1:T(8,128)}) %all-reduce.7.cloned.1.call-update) | async-done | bytes 1048592 | tf_op jit(solution)/shard_map/psum | solution.py:104
  142.8 14.6 %all-reduce.3 = (f32[]{:T(128)}, f32[512]{0:T(512)S(1)}) all-reduce(f32[]{:T(128)} %dynamic-slice_reduce_fusion, f32[512]{0:T(512)S(1)} %get-tuple-element.82), channel_id=1, replica_groups=mesh['rows'=64,'cols'=8] {'cols'}, use_global_device_ids=true, to_apply=%region_10.0 | all-reduce | flops 513 | bytes 4104 | tf_op jit(solution)/shard_map/psum | solution.py:104
  157.4 117.2 %all-reduce.2 = (f32[]{:T(128)}, f32[512]{0:T(512)S(1)}) all-reduce(f32[]{:T(128)} %get-tuple-element.149, f32[512]{0:T(512)S(1)} %get-tuple-element.150), channel_id=1, replica_groups=mesh['rows'=64,'cols'=8] {'rows'}, use_global_device_ids=true, to_apply=%region_11.0 | all-reduce | flops 513 | bytes 4104 | tf_op jit(solution)/shard_map/psum | solution.py:103
  275.3 134.7 %all-reduce.9.cloned.1.call-done = f32[512,512]{0,1:T(8,128)} async-done(((f32[512,512]{0,1:T(8,128)}), f32[512,512]{0,1:T(8,128)}) %all-reduce.9.cloned.1.call-update) | async-done | bytes 1048592 | tf_op jit(solution)/shard_map/psum | solution.py:103
  410.0 2.0 select_add_fusion
  412.3 2.1 fusion.12
  414.5 11.7 %cholesky.103 = f32[128,128]{1,0:T(8,128)S(1)} custom-call(f32[128,128]{1,0:T(8,128)S(1)} %cholesky.263), custom_call_target="Cholesky" | custom-call | tf_op jit(solution)/shard_map/jit(cholesky)/cholesky | solution.py:107
  426.2 9.8 %custom-call.32 = f32[1,128,128]{1,2,0:T(8,128)S(1)} custom-call(f32[1,128,128]{2,1,0:T(8,128)S(1)} %get-tuple-element.164), custom_call_target="InvertDiagBlocksLowerTriangular" | custom-call | tf_op jit(solution)/shard_map/jit(cholesky)/cholesky | solution.py:107
  436.7 11.7 %cholesky.215 = f32[128,128]{1,0:T(8,128)S(1)} custom-call(f32[128,128]{1,0:T(8,128)S(1)} %cholesky.267), custom_call_target="Cholesky" | custom-call | tf_op jit(solution)/shard_map/jit(cholesky)/cholesky | solution.py:107
  448.9 9.9 %custom-call.33 = f32[1,128,128]{1,2,0:T(8,128)S(1)} custom-call(f32[1,128,128]{2,1,0:T(8,128)S(1)} %get-tuple-element.162), custom_call_target="InvertDiagBlocksLowerTriangular" | custom-call | tf_op jit(solution)/shard_map/jit(cholesky)/cholesky | solution.py:107
  459.9 11.7 %cholesky.236 = f32[128,128]{1,0:T(8,128)S(1)} custom-call(f32[128,128]{1,0:T(8,128)S(1)} %cholesky.272), custom_call_target="Cholesky" | custom-call | tf_op jit(solution)/shard_map/jit(cholesky)/cholesky | solution.py:107
  471.7 9.8 %custom-call.34 = f32[1,128,128]{1,2,0:T(8,128)S(1)} custom-call(f32[1,128,128]{2,1,0:T(8,128)S(1)} %get-tuple-element.160), custom_call_target="InvertDiagBlocksLowerTriangular" | custom-call | tf_op jit(solution)/shard_map/jit(cholesky)/cholesky | solution.py:107
  482.3 11.9 %cholesky.253 = f32[128,128]{1,0:T(8,128)S(1)} custom-call(f32[128,128]{1,0:T(8,128)S(1)} %convolution_subtract_fusion.2), custom_call_target="Cholesky" | custom-call | tf_op jit(solution)/shard_map/jit(cholesky)/cholesky | solution.py:107
  500.1 11.3 %while.16 = (s32[]{:T(128)}, f32[512,512]{0,1:T(8,128)S(1)}, s32[4,2]{0,1:T(2,128)S(1)}, f32[4,128,128]{2,1,0:T(8,128)}, s32[]{:T(128)}) while((s32[]{:T(128)}, f32[512,512]{0,1:T(8,128)S(1)}, s32[4,2]{0,1:T(2,128)S(1)}, f32[4,128,128]{2,1,0:T(8,128)}, s32[]{:T(128)}) %tuple.61), condition=%wide.while_cond, body=%wide.while_body.sunk | while | flops 2 | bytes 393829 | solution.py:53
  500.8 1.4 dynamic-slice.12
  503.6 1.4 dynamic-slice.12
  506.5 1.4 dynamic-slice.12
  509.3 1.4 dynamic-slice.12
  511.4 40.1 %custom-call.35 = f32[4,128,128]{1,2,0:T(8,128)S(1)} custom-call(f32[4,128,128]{2,1,0:T(8,128)} %get-tuple-element.90), custom_call_target="InvertDiagBlocksLowerTriangular" | custom-call | tf_op jit(solution)/shard_map/triangular_solve | solution.py:53
  556.1 22.7 %all-reduce.1 = f32[2048]{0:T(1024)S(1)} all-reduce(f32[2048]{0:T(1024)S(1)} %bitcast.197), channel_id=2, replica_groups=mesh['rows'=64,'cols'=8] {'cols'}, use_global_device_ids=true, to_apply=%region_22.23.clone | all-reduce | flops 2048 | bytes 16384
  (128 shorter events, 36.0 us)
Async XLA Ops:
  7.2 9.1 %copy-start = (f32[8,32,128]{2,1,0:T(8,128)S(1)}, f32[8,32,128]{2,1,0:T(8,128)}, u32[]{:S(2)}) copy-start(f32[8,32,128]{2,1,0:T(8,128)} %param.10) | copy-start | bytes 393220
  7.2 31.7 %copy-start.1 = (f32[64,8]{0,1:T(8,128)S(1)}, f32[64,8]{0,1:T(8,128)}, u32[]{:S(2)}) copy-start(f32[64,8]{0,1:T(8,128)} %param.15) | copy-start | bytes 6148
  7.2 33.0 %copy-start.3 = (f32[64]{0:T(128)S(1)}, f32[64]{0:T(128)}, u32[]{:S(2)}) copy-start(f32[64]{0:T(128)} %param.16) | copy-start | bytes 772
  7.2 33.1 %copy-start.2 = (s32[2048]{0:T(1024)S(1)}, s32[2048]{0:T(1024)}, u32[]{:S(2)}) copy-start(s32[2048]{0:T(1024)} %param.12) | copy-start | bytes 24580
  41.5 19.6 %all-to-all-start = ((f32[8,256,64]{1,2,0:T(8,128)}), f32[8,256,64]{1,2,0:T(8,128)S(1)}, u32[]{:S(2)}, u32[]{:S(2)}) async-start(f32[8,256,64]{1,2,0:T(8,128)} %copy.43), calls=%async_computation | async-start | bytes 1048576 | tf_op jit(solution)/shard_map/all_to_all | solution.py:85
  51.8 87.7 %all-reduce.7.cloned.1.call-start = ((), (), s32[]{:S(2)}) async-start(), calls=%async_computation.1 | async-start | bytes 2097152 | tf_op jit(solution)/shard_map/psum | solution.py:104
  64.5 345.5 %all-reduce.9.cloned.1.call-start = ((), (), s32[]{:S(2)}) async-start(), calls=%async_computation.2 | async-start | bytes 2097152 | tf_op jit(solution)/shard_map/psum | solution.py:103
Sparse Core Ops, SparseCore 0:
  64.6 74.7 all-reduce.6
  142.8 267.1 all-reduce.8
